TPU v7x, 32 devices: a whole 2x2x4 slice. The times are simulated.
32 devices in a mesh: rep: 4 (over x, core), row: 4 (over z), col: 2 (over y).
Axes of the slice: x: 2, y: 2, z: 4, core: 2. Of those that a mesh axis runs over, the one named last changes fastest.
Arguments:
- inputs: bfloat16 [4, 128, 6144], P('rep', 'col', 'row'), may hold values from -6 to 6
- w_in: bfloat16 [6144, 24576], P('row', ('rep', 'col')), may hold values from -0.078125 to 0.078125
- w_out: bfloat16 [24576, 6144], P(('rep', 'col'), 'row'), may hold values from -0.0390625 to 0.0390625
- cotangent: bfloat16 [4, 128, 6144], P('rep', 'col', 'row'), may hold values from -1536 to 1536
- counts: int32 [4], replicated, may hold values from 0 to 4, as said below
Outputs:
- block_output: bfloat16 [4, 128, 6144], P('rep', 'col', 'row')
- input_grad: bfloat16 [4, 128, 6144], P('rep', 'col', 'row')
- w_in_grad: float32 [6144, 24576], P('row', ('rep', 'col'))
- w_out_grad: float32 [24576, 6144], P(('rep', 'col'), 'row')
Inputs may be any that keep to these rules, and one draw needn't show every extreme that they name: Replica r completed its first counts[r] micro-batches; at least one replica completed all 4.
All inputs are finite; a program needn't handle non-finite values.
Results may differ from a plain program's by a relative error of at most 0.015.
Values may be sent and summed in bfloat16 or wider, within the bound.
A program may use at most 192 MiB of HBM per device.

v0:
```python
import jax
import jax.numpy as jnp
from jax import lax
from jax.sharding import PartitionSpec as P

MBT = 32


root_coef = 0.7978845608028654
cubic_coef = 0.044715


def gelu_tanh(values):
    inner = root_coef * (values + cubic_coef * values * values * values)
    return 0.5 * values * (1.0 + jnp.tanh(inner))


def gelu_slope(values):
    inner = root_coef * (values + cubic_coef * values * values * values)
    tangent = jnp.tanh(inner)
    return 0.5 * (1.0 + tangent) + 0.5 * values * (1.0 - tangent * tangent) * root_coef * (
        1.0 + 3.0 * cubic_coef * values * values
    )


def right_product(left, right):
    return lax.dot_general(
        left, right, (((1,), (1,)), ((), ())), preferred_element_type=jnp.float32
    )


def first_product(left, right):
    return lax.dot_general(
        left, right, (((0,), (0,)), ((), ())), preferred_element_type=jnp.float32
    )


def bits_of(axis):
    size, bits = lax.axis_size(axis), []
    while size > 1:
        size //= 2
        bits.append(size)
    return bits


def swapped(values, axis, bit):
    pairs = [(i, i ^ bit) for i in range(lax.axis_size(axis))]
    return lax.ppermute(values, axis, pairs)


def doubling_gather(rows, axis):
    for bit in reversed(bits_of(axis)):
        other = swapped(rows, axis, bit)
        upper = (lax.axis_index(axis) // bit) % 2 == 1
        rows = jnp.concatenate(
            [jnp.where(upper, other, rows), jnp.where(upper, rows, other)], axis=0
        )
    return rows


def halving_sum(terms, axis):
    total = terms
    for bit in bits_of(axis):
        half = total.shape[0] // 2
        upper = (lax.axis_index(axis) // bit) % 2 == 1
        low, high = total[:half], total[half:]
        sent = jnp.where(upper, low, high).astype(jnp.bfloat16)
        other = swapped(sent, axis, bit)
        total = jnp.where(upper, high, low).astype(jnp.float32) + other.astype(jnp.float32)
    return total


def body(inputs, w_in, w_out, cotangent, counts):
    rows_local = inputs.shape[1]
    width_local = inputs.shape[2]
    tokens_local = inputs.reshape(rows_local, width_local)
    replicas = lax.axis_size("rep")
    replica_index = lax.axis_index("rep")
    column_index = lax.axis_index("col")
    own_count = jnp.sum(jnp.where(jnp.arange(replicas) == replica_index, counts, 0))
    token_total = (MBT * jnp.sum(counts)).astype(jnp.float32)
    positions = column_index * rows_local + jnp.arange(rows_local, dtype=jnp.int32)
    kept_mask = (positions // MBT < own_count).astype(jnp.float32)
    scaled = (
        cotangent.reshape(rows_local, width_local).astype(jnp.float32)
        * kept_mask[:, None]
        / token_total
    ).astype(jnp.bfloat16)
    tokens_all = lax.all_gather(tokens_local, ("rep", "col"), axis=0, tiled=True)
    scaled_all = doubling_gather(doubling_gather(scaled, "col"), "rep")
    partial_hidden = jnp.dot(tokens_all, w_in, preferred_element_type=jnp.float32)
    hidden = lax.psum_scatter(
        partial_hidden.astype(jnp.bfloat16), "row", scatter_dimension=0, tiled=True
    ).astype(jnp.float32)
    slope_terms = right_product(scaled_all, w_out)
    slope_sum = lax.psum_scatter(
        slope_terms.astype(jnp.bfloat16), "row", scatter_dimension=0, tiled=True
    ).astype(jnp.float32)
    active_share = gelu_tanh(hidden).astype(jnp.bfloat16)
    activated = lax.all_gather(active_share, "row", axis=0, tiled=True)
    grad_share = (slope_sum * gelu_slope(hidden)).astype(jnp.bfloat16)
    hidden_grad = lax.all_gather(grad_share, "row", axis=0, tiled=True)
    output_terms = jnp.dot(activated, w_out, preferred_element_type=jnp.float32)
    output_local = halving_sum(halving_sum(output_terms.astype(jnp.bfloat16), "rep"), "col")
    block_output = (tokens_local.astype(jnp.float32) + output_local).astype(jnp.bfloat16)
    w_out_grad = first_product(activated, scaled_all)
    back_terms = right_product(hidden_grad, w_in)
    back_local = halving_sum(halving_sum(back_terms.astype(jnp.bfloat16), "rep"), "col")
    input_grad = (scaled.astype(jnp.float32) + back_local).astype(jnp.bfloat16)
    w_in_grad = first_product(tokens_all, hidden_grad)
    return (
        block_output.reshape(1, rows_local, width_local),
        input_grad.reshape(1, rows_local, width_local),
        w_in_grad,
        w_out_grad,
    )


def solution(mesh):
    placed = (
        P("rep", "col", "row"),
        P("row", ("rep", "col")),
        P(("rep", "col"), "row"),
        P("rep", "col", "row"),
        P(),
    )
    return jax.shard_map(
        body,
        mesh=mesh,
        in_specs=placed,
        out_specs=(
            P("rep", "col", "row"),
            P("rep", "col", "row"),
            P("row", ("rep", "col")),
            P(("rep", "col"), "row"),
        ),
        check_vma=False,
    )
```

profile of v0, /device:TPU:0, one launch (start us, length us, event | category | flops | bytes accessed | tf_op | source)
XLA Modules:
  0.0 389.7 jit_solution(1617677210352436067)
XLA Ops:
  8.0 0.0 all-gather.9.cloned.1.call-start
  8.0 1.3 fusion.19
  10.0 0.7 compare_convert_fusion
  10.7 1.0 fusion.15
  11.7 3.1 collective-permute-start.3
  14.8 4.9 %collective-permute-done.3 = bf16[64,1536]{1,0:T(8,128)(2,1)S(1)} collective-permute-done((bf16[64,1536]{1,0:T(8,128)(2,1)S(1)}, bf16[64,1536]{1,0:T(8,128)(2,1)S(1)}, u32[]{:S(2)}, u32[]{:S(2)}) %collective-permute-start.3) | collective-permute-done | bytes 196640 | tf_op jit(solution)/shard_map/ppermute | solution.py:48
  19.7 1.1 broadcast_select_fusion.7
  20.8 0.1 collective-permute-start.4
  20.9 0.0 all-gather.9.cloned.1.call-update
  20.9 0.0 reduce-scatter.5.cloned.1.call-start
  21.0 1.6 collective-permute-done.4
  22.6 0.1 broadcast_select_fusion.5
  22.7 0.1 pad_maximum_fusion.3
  22.8 1.8 collective-permute-start.5
  24.6 21.3 %collective-permute-done.5 = bf16[256,1536]{1,0:T(8,128)(2,1)S(1)} collective-permute-done((bf16[256,1536]{1,0:T(8,128)(2,1)S(1)}, bf16[256,1536]{1,0:T(8,128)(2,1)S(1)}, u32[]{:S(2)}, u32[]{:S(2)}) %collective-permute-start.5) | collective-permute-done | bytes 786464 | tf_op jit(solution)/shard_map/ppermute | solution.py:48
  45.9 0.3 broadcast_select_fusion.2
  46.1 0.0 copy-start.2
  46.2 0.9 copy-done.2
  47.1 0.3 copy-done.3
  47.4 10.5 %convolution_convert_fusion = bf16[512,3072]{1,0:T(8,128)(2,1)} fusion(bf16[3072,1536]{1,0:T(8,128)(2,1)} %param.7, bf16[256,1536]{1,0:T(8,128)(2,1)S(1)} %get-tuple-element.11, bf16[256,1536]{1,0:T(8,128)(2,1)S(1)} %get-tuple-element.10), kind=kOutput, calls=%fused_computation.1 | convolution fusion | flops 4836556800 | bytes 14155776 | tf_op jit(solution)/shard_map/dot_general | solution.py:27
  57.9 0.0 reduce-scatter.5.cloned.1.call-update
  57.9 0.0 reduce-scatter.3.cloned.1.call-start
  58.0 0.0 all-gather.9.cloned.1.call-done
  58.0 9.2 %convolution_convert_fusion.1 = bf16[512,3072]{1,0:T(8,128)(2,1)} fusion(bf16[1536,3072]{1,0:T(8,128)(2,1)} %param.6, bf16[1,512,1536]{2,1,0:T(8,128)(2,1)} %all-gather.9.cloned.1.call-done), kind=kOutput, calls=%fused_computation.2 | convolution fusion | flops 4833411072 | bytes 14155776 | tf_op jit(solution)/shard_map/dot_general | solution.py:91
  67.2 0.0 reduce-scatter.3.cloned.1.call-update
  67.2 0.0 all-gather.5.cloned.1.call-start
  67.3 53.4 %reduce-scatter.5.cloned.1.call-done = bf16[128,3072]{1,0:T(8,128)(2,1)} async-done(((bf16[512,3072]{1,0:T(8,128)(2,1)}), bf16[128,3072]{1,0:T(8,128)(2,1)}) %reduce-scatter.5.cloned.1.call-update) | async-done | bytes 786448 | tf_op jit(solution)/shard_map/reduce_scatter | solution.py:96
  120.7 63.0 %reduce-scatter.3.cloned.1.call-done = bf16[128,3072]{1,0:T(8,128)(2,1)} async-done(((bf16[512,3072]{1,0:T(8,128)(2,1)}), bf16[128,3072]{1,0:T(8,128)(2,1)}) %reduce-scatter.3.cloned.1.call-update) | async-done | bytes 786448 | tf_op jit(solution)/shard_map/reduce_scatter | solution.py:92
  183.7 3.7 fusion.7
  187.4 0.0 all-gather.5.cloned.1.call-update
  187.4 0.2 all-gather.7.cloned.1.call-start
  187.6 0.5 all-gather.7.cloned.1.call-update
  188.1 62.5 %all-gather.5.cloned.1.call-done = bf16[512,3072]{1,0:T(8,128)(2,1)} async-done(((bf16[128,3072]{1,0:T(8,128)(2,1)}), bf16[512,3072]{1,0:T(8,128)(2,1)}) %all-gather.5.cloned.1.call-update) | async-done | bytes 3145744 | tf_op jit(solution)/shard_map/all_gather | solution.py:100
  250.6 9.4 %convolution_convert_fusion.3 = bf16[512,1536]{1,0:T(8,128)(2,1)S(1)} fusion(bf16[512,3072]{1,0:T(8,128)(2,1)} %all-gather.5.cloned.1.call-done, bf16[3072,1536]{1,0:T(8,128)(2,1)} %param.7), kind=kOutput, calls=%fused_computation.11 | convolution fusion | flops 4832624640 | bytes 14155776 | tf_op jit(solution)/shard_map/dot_general | solution.py:103
  260.0 1.0 broadcast_select_fusion.3
  261.0 1.5 collective-permute-start
  262.5 52.3 %all-gather.7.cloned.1.call-done = bf16[512,3072]{1,0:T(8,128)(2,1)} async-done(((bf16[128,3072]{1,0:T(8,128)(2,1)}), bf16[512,3072]{1,0:T(8,128)(2,1)}) %all-gather.7.cloned.1.call-update) | async-done | bytes 3145744 | tf_op jit(solution)/shard_map/all_gather | solution.py:102
  314.8 9.6 %convolution_convert_fusion.2 = bf16[512,1536]{1,0:T(8,128)(2,1)S(1)} fusion(bf16[512,3072]{1,0:T(8,128)(2,1)} %all-gather.7.cloned.1.call-done, bf16[1536,3072]{1,0:T(8,128)(2,1)} %param.6), kind=kOutput, calls=%fused_computation.10 | convolution fusion | flops 4832624640 | bytes 14155776 | tf_op jit(solution)/shard_map/dot_general | solution.py:27
  324.4 0.9 broadcast_select_fusion
  325.4 1.5 collective-permute-start.6
  326.8 0.0 copy-done.5
  326.8 9.5 %convolution_bitcast_fusion = f32[1536,3072]{0,1:T(8,128)} fusion(bf16[512,3072]{1,0:T(8,128)(2,1)S(1)} %copy-done.4, bf16[1,512,1536]{2,1,0:T(8,128)(2,1)S(1)} %copy-done.5), kind=kOutput, calls=%fused_computation | convolution fusion | flops 4831838208 | bytes 23592960 | tf_op jit(solution)/shard_map/dot_general | solution.py:33
  336.3 18.6 %copy.9 = f32[1536,3072]{1,0:T(8,128)} copy(f32[1536,3072]{0,1:T(8,128)} %convolution_bitcast_fusion) | data formatting | bytes 37748736
  355.0 11.4 %fusion.13 = f32[3072,1536]{1,0:T(8,128)} fusion(bf16[512,3072]{1,0:T(8,128)(2,1)} %all-gather.5.cloned.1.call-done, bf16[256,1536]{1,0:T(8,128)(2,1)} %copy-done.3, bf16[256,1536]{1,0:T(8,128)(2,1)} %copy-done.2), kind=kOutput, calls=%fused_computation.28 | convolution fusion | flops 4834983936 | bytes 23592960 | tf_op jit(solution)/shard_map/dot_general | solution.py:33
  366.3 0.0 collective-permute-done
  366.3 1.4 convert_add_fusion.2
  367.8 0.1 select_convert_fusion.1
  367.8 0.1 collective-permute-start.1
  367.9 0.0 collective-permute-done.6
  367.9 1.4 convert_add_fusion.1
  369.4 0.1 select_convert_fusion
  369.4 0.6 collective-permute-start.7
  370.0 0.0 collective-permute-done.1
  370.0 0.1 convert_add_fusion.4
  370.2 0.0 copy-start.1
  370.2 1.5 collective-permute-start.2
  371.7 0.0 collective-permute-done.7
  371.7 0.1 convert_add_fusion.3
  371.9 0.0 copy-start
  371.9 1.2 collective-permute-start.8
  373.1 4.9 %collective-permute-done.2 = bf16[64,1536]{1,0:T(8,128)(2,1)S(1)} collective-permute-done((bf16[64,1536]{1,0:T(8,128)(2,1)S(1)}, bf16[64,1536]{1,0:T(8,128)(2,1)S(1)}, u32[]{:S(2)}, u32[]{:S(2)}) %collective-permute-start.2) | collective-permute-done | bytes 196640 | tf_op jit(solution)/shard_map/ppermute | solution.py:48
  378.0 0.8 fusion.18
  378.8 2.5 collective-permute-done.8
  381.3 0.8 fusion.17
  (9 shorter events, 0.1 us)
Async XLA Ops:
  8.0 50.0 %all-gather.9.cloned.1.call-start = ((), (), s32[]{:S(2)}) async-start(), calls=%async_computation.6 | async-start | bytes 1769472 | tf_op jit(solution)/shard_map/all_gather | solution.py:89
  11.7 8.0 %collective-permute-start.3 = (bf16[64,1536]{1,0:T(8,128)(2,1)S(1)}, bf16[64,1536]{1,0:T(8,128)(2,1)S(1)}, u32[]{:S(2)}, u32[]{:S(2)}) collective-permute-start(bf16[64,1536]{1,0:T(8,128)(2,1)S(1)} %fusion.15), channel_id=1, source_target_pairs={{0,1},{1,0},{2,3},{3,2},{4,5},{5,4},{6,7},{7,6},{8,9},{9,8},{10,11... | collective-permute-start | bytes 589832 | tf_op jit(solution)/shard_map/ppermute | solution.py:48
  20.8 1.8 collective-permute-start.4
  20.9 99.7 %reduce-scatter.5.cloned.1.call-start = ((), (), s32[]{:S(2)}) async-start(), calls=%async_computation.4 | async-start | bytes 3932160 | tf_op jit(solution)/shard_map/reduce_scatter | solution.py:96
  22.8 23.1 %collective-permute-start.5 = (bf16[256,1536]{1,0:T(8,128)(2,1)S(1)}, bf16[256,1536]{1,0:T(8,128)(2,1)S(1)}, u32[]{:S(2)}, u32[]{:S(2)}) collective-permute-start(bf16[256,1536]{1,0:T(8,128)(2,1)S(1)} %pad_maximum_fusion.3), channel_id=1, source_target_pairs={{0,16},{8,24},{16,0},{24,8},{1,17},{9,25},{17,1},{25,9},{2,18},{10... | collective-permute-start | bytes 2359304 | tf_op jit(solution)/shard_map/ppermute | solution.py:48
  46.1 0.9 copy-start.2
  46.2 1.2 copy-start.3
  57.9 125.8 %reduce-scatter.3.cloned.1.call-start = ((), (), s32[]{:S(2)}) async-start(), calls=%async_computation.2 | async-start | bytes 3932160 | tf_op jit(solution)/shard_map/reduce_scatter | solution.py:92
  67.2 183.4 %all-gather.5.cloned.1.call-start = ((), (), s32[]{:S(2)}) async-start(), calls=%async_computation.3 | async-start | bytes 3932160 | tf_op jit(solution)/shard_map/all_gather | solution.py:100
  187.4 127.4 %all-gather.7.cloned.1.call-start = ((), (), s32[]{:S(2)}) async-start(), calls=%async_computation.5 | async-start | bytes 3932160 | tf_op jit(solution)/shard_map/all_gather | solution.py:102
  261.0 105.3 %collective-permute-start = (bf16[256,1536]{1,0:T(8,128)(2,1)}, bf16[256,1536]{1,0:T(8,128)(2,1)}, u32[]{:S(2)}, u32[]{:S(2)}) collective-permute-start(bf16[256,1536]{1,0:T(8,128)(2,1)} %broadcast_select_fusion.3), channel_id=1, source_target_pairs={{0,16},{8,24},{16,0},{24,8},{1,17},{9,25},{17,1},{25,9},{2,18},{10... | collective-permute-start | bytes 2359304 | tf_op jit(solution)/shard_map/ppermute | solution.py:48
  314.8 12.0 %copy-start.4 = (bf16[512,3072]{1,0:T(8,128)(2,1)S(1)}, bf16[512,3072]{1,0:T(8,128)(2,1)}, u32[]{:S(2)}) copy-start(bf16[512,3072]{1,0:T(8,128)(2,1)} %all-gather.7.cloned.1.call-done) | copy-start | bytes 9437188
  324.4 2.4 copy-start.5
  325.4 42.6 %collective-permute-start.6 = (bf16[256,1536]{1,0:T(8,128)(2,1)}, bf16[256,1536]{1,0:T(8,128)(2,1)}, u32[]{:S(2)}, u32[]{:S(2)}) collective-permute-start(bf16[256,1536]{1,0:T(8,128)(2,1)} %broadcast_select_fusion), channel_id=1, source_target_pairs={{0,16},{8,24},{16,0},{24,8},{1,17},{9,25},{17,1},{25,9},{2,18},{10... | collective-permute-start | bytes 2359304 | tf_op jit(solution)/shard_map/ppermute | solution.py:48
  367.8 2.2 collective-permute-start.1
  369.4 2.3 collective-permute-start.7
  370.2 7.9 %copy-start.1 = (bf16[1,64,1536]{2,1,0:T(8,128)(2,1)S(1)}, bf16[1,64,1536]{2,1,0:T(8,128)(2,1)}, u32[]{:S(2)}) copy-start(bf16[1,64,1536]{2,1,0:T(8,128)(2,1)} %param.5) | copy-start | bytes 589828
  370.2 7.8 %collective-permute-start.2 = (bf16[64,1536]{1,0:T(8,128)(2,1)S(1)}, bf16[64,1536]{1,0:T(8,128)(2,1)S(1)}, u32[]{:S(2)}, u32[]{:S(2)}) collective-permute-start(bf16[64,1536]{1,0:T(8,128)(2,1)S(1)} %select_convert_fusion.3), channel_id=1, source_target_pairs={{0,1},{1,0},{2,3},{3,2},{4,5},{5,4},{6,7},{7,6},{8,9},{9,8},{10,11... | collective-permute-start | bytes 589832 | tf_op jit(solution)/shard_map/ppermute | solution.py:48
  371.9 9.4 %copy-start = (bf16[1,64,1536]{2,1,0:T(8,128)(2,1)S(1)}, bf16[1,64,1536]{2,1,0:T(8,128)(2,1)}, u32[]{:S(2)}) copy-start(bf16[1,64,1536]{2,1,0:T(8,128)(2,1)} %param.8) | copy-start | bytes 589828
  371.9 9.4 %collective-permute-start.8 = (bf16[64,1536]{1,0:T(8,128)(2,1)S(1)}, bf16[64,1536]{1,0:T(8,128)(2,1)S(1)}, u32[]{:S(2)}, u32[]{:S(2)}) collective-permute-start(bf16[64,1536]{1,0:T(8,128)(2,1)S(1)} %select_convert_fusion.2), channel_id=1, source_target_pairs={{0,1},{1,0},{2,3},{3,2},{4,5},{5,4},{6,7},{7,6},{8,9},{9,8},{10,11... | collective-permute-start | bytes 589832 | tf_op jit(solution)/shard_map/ppermute | solution.py:48
Sparse Core Ops, SparseCore 0:
  21.0 29.3 all-gather.8
Sparse Core Ops, SparseCore 1:
  58.0 62.6 reduce-scatter.4
  123.4 60.2 reduce-scatter.2
  187.5 63.1 all-gather.4
  252.8 61.9 all-gather.6
where the time goes:
time: 390 us
  waiting for transfers between devices  267 us (68%)
  matrix products  59.6 us (15%)
  local copies, waits for them, and re-layouts  19.9 us (5%)
  between operations  16.6 us (4%)
  other arithmetic  15 us (4%)
  starting transfers between devices  11.6 us (3%)
    reduce_scatter x1, waiting for transfers between devices, body(): lax.psum_scatter(partial_hidden.astype(jnp.bfloat16), 'row', scatter_dime...  63 us
    all_gather x1, waiting for transfers between devices, body(): activated = lax.all_gather(active_share, 'row', axis=0, tiled=True)  62.5 us
    reduce_scatter x1, waiting for transfers between devices, body(): lax.psum_scatter(slope_terms.astype(jnp.bfloat16), 'row', scatter_dimensi...  53.4 us
    all_gather x1, waiting for transfers between devices, body(): hidden_grad = lax.all_gather(grad_share, 'row', axis=0, tiled=True)  52.3 us
    ppermute x9, waiting for transfers between devices, swapped(): return lax.ppermute(values, axis, pairs)  35.3 us
    dot_general x2, matrix products, first_product(): lax.dot_general(left, right, (((0,), (0,)), ((), ())), preferred_element_...  20.9 us
    dot_general x2, matrix products, right_product(): lax.dot_general(left, right, (((1,), (1,)), ((), ())), preferred_element_...  20.1 us
    unnamed x13, local copies, waits for them, and re-layouts  19.9 us
  transfers between devices with their start and end apart: 14, of which 9 were waited for; matrix products, arithmetic and copies ran while one was open for 22% of the time, Pallas kernels for 0%

commit v1 on v0

v1 whole, which is shorter than its diff:
```python
import functools

import jax
import jax.numpy as jnp
from jax import lax
from jax.experimental import pallas as pl
from jax.experimental.pallas import tpu as pltpu
from jax.sharding import PartitionSpec as P

MBT = 32
HALF = 128
GROUP = 2 * HALF
LAG = 2
MESH = pl.DeviceIdType.MESH

root_coef = 0.7978845608028654
cubic_coef = 0.044715


def gelu_tanh(values):
    inner = root_coef * (values + cubic_coef * values * values * values)
    return 0.5 * values * (1.0 + jnp.tanh(inner))


def gelu_slope(values):
    inner = root_coef * (values + cubic_coef * values * values * values)
    tangent = jnp.tanh(inner)
    return 0.5 * (1.0 + tangent) + 0.5 * values * (1.0 - tangent * tangent) * root_coef * (
        1.0 + 3.0 * cubic_coef * values * values
    )


def wide(values):
    return values.astype(jnp.float32)


def narrow(values):
    return values.astype(jnp.bfloat16)


def product(left, right):
    return jnp.dot(left, right, preferred_element_type=jnp.float32)


def right_product(left, right):
    return lax.dot_general(
        left, right, (((1,), (1,)), ((), ())), preferred_element_type=jnp.float32
    )


def first_product(left, right):
    return lax.dot_general(
        left, right, (((0,), (0,)), ((), ())), preferred_element_type=jnp.float32
    )


def rows_at(start, size):
    return pl.ds(pl.multiple_of(start, size), size)


def step_kernel(
    sizes,
    counts, x_ref, cot_ref, w1_hbm, w2_hbm,
    bo_ref, ig_ref, act_hbm, grad_hbm, xa_hbm, sa_hbm,
    w1, w2, xa, sa, scaled,
    part, came, result,
    acc, pair_out, pair_in, chip_out, chip_in,
    w_sem, near_send, near_recv, pair_send, pair_recv,
    part_send, part_recv, res_send, res_recv, out_sem,
    pair2_send, pair2_recv, chip_send, chip_recv,
):
    n_rep, n_row, n_col, tl, width, hidden, groups = sizes
    total_rows = n_rep * n_col * tl
    halves = hidden // HALF
    rep, row, col = (lax.axis_index(name) for name in ("rep", "row", "col"))
    core, chip = lax.rem(rep, 2), rep // 2
    n_chip = n_rep // 2
    partner = rep + 1 - 2 * core
    block = rep * n_col + col
    offsets = [(i, j) for i in range(n_chip) for j in range(n_col) if i + j > 0]
    near = len(offsets)

    def to_of(i, j):
        return lax.rem(chip + i, n_chip), lax.rem(col + j, n_col)

    def from_of(i, j):
        return lax.rem(chip + n_chip - i, n_chip), lax.rem(col + n_col - j, n_col)

    def block_rows(chip_at, core_at, col_at):
        return rows_at(((2 * chip_at + core_at) * n_col + col_at) * tl, tl)

    def each(count, body):
        lax.fori_loop(0, count, lambda i, c: (body(i), c)[1], 0)

    def size_of(i):
        return min(GROUP, hidden - i * GROUP)

    def w1_copy(i):
        return pltpu.make_async_copy(
            w1_hbm.at[:, pl.ds(i * GROUP, size_of(i))],
            w1.at[i, :, pl.ds(0, size_of(i))],
            w_sem.at[0, i],
        )

    def w2_copy(i):
        return pltpu.make_async_copy(
            w2_hbm.at[pl.ds(i * GROUP, size_of(i)), :],
            w2.at[i, pl.ds(0, size_of(i)), :],
            w_sem.at[1, i],
        )

    for i in range(groups):
        if size_of(i) < GROUP:
            w1[i, :, size_of(i):] = jnp.zeros((width, GROUP - size_of(i)), jnp.bfloat16)
            w2[i, size_of(i):, :] = jnp.zeros((GROUP - size_of(i), width), jnp.bfloat16)
        w1_copy(i).start()
    for i in range(groups):
        w2_copy(i).start()

    barrier = pltpu.get_barrier_semaphore()
    for i, j in offsets:
        chip_at, col_at = to_of(i, j)
        pl.semaphore_signal(
            barrier, inc=1, device_id=(2 * chip_at + core, row, col_at), device_id_type=MESH
        )
    pl.semaphore_signal(barrier, inc=1, device_id=(partner, row, col), device_id_type=MESH)

    @pl.when(row > 0)
    def _():
        pl.semaphore_signal(barrier, inc=1, device_id=(rep, row - 1, col), device_id_type=MESH)

    @pl.when(row < n_row - 1)
    def _():
        pl.semaphore_signal(barrier, inc=1, device_id=(rep, row + 1, col), device_id_type=MESH)

    at_ends = jnp.where(row > 0, 1, 0) + jnp.where(row < n_row - 1, 1, 0)
    pl.semaphore_wait(barrier, near + 1 + at_ends)

    def near_copy(which, source, target, k):
        i, j = offsets[k]
        chip_at, col_at = to_of(i, j)
        return pltpu.make_async_remote_copy(
            src_ref=source,
            dst_ref=target.at[block_rows(chip, core, col), :],
            send_sem=near_send.at[which, k],
            recv_sem=near_recv.at[which, k],
            device_id=(2 * chip_at + core, row, col_at),
            device_id_type=MESH,
        )

    def pair_copy(which, source, target, k):
        rows = block_rows(chip, core, col)
        if k < near:
            chip_at, col_at = from_of(*offsets[k])
            rows = block_rows(chip_at, core, col_at)
            source = target.at[rows, :]
        return pltpu.make_async_remote_copy(
            src_ref=source,
            dst_ref=target.at[rows, :],
            send_sem=pair_send.at[which, k],
            recv_sem=pair_recv.at[which, k],
            device_id=(partner, row, col),
            device_id_type=MESH,
        )

    def gather_start(which, source, target):
        for k in range(near):
            near_copy(which, source, target, k).start()
        pair_copy(which, source, target, near).start()

    def gather_pass(which, source, target):
        for k in range(near):
            near_copy(which, source, target, k).wait_recv()
            pair_copy(which, source, target, k).start()

    def gather_end(which, source, target):
        for k in range(near + 1):
            pair_copy(which, source, target, k).wait_recv()

    gather_start(0, x_ref, xa)
    own = block_rows(chip, core, col)
    xa[own, :] = x_ref[...]
    kept_rows = MBT * counts[rep]
    counted = counts[0]
    for r in range(1, n_rep):
        counted = counted + counts[r]
    token_total = (MBT * counted).astype(jnp.float32)
    position = col * tl + lax.broadcasted_iota(jnp.int32, (tl, width), 0)
    kept = jnp.where(position < kept_rows, 1.0, 0.0)
    value = narrow(wide(cot_ref[...]) * kept / token_total)
    scaled[...] = value
    sa[own, :] = value
    gather_pass(0, x_ref, xa)
    gather_start(1, scaled, sa)
    gather_end(0, x_ref, xa)

    kinds = 2
    result_tick = max(kinds * groups, (n_row - 1) * LAG + 1)
    use_tick = result_tick + (n_row - 1) * LAG
    ticks = use_tick + kinds * groups
    places = (row, n_row - 1 - row)
    nexts = (row + 1, row - 1)

    def part_copy(kind, i, d):
        return pltpu.make_async_remote_copy(
            src_ref=part.at[kind, i, d],
            dst_ref=came.at[kind, i, d],
            send_sem=part_send.at[kind, i, d],
            recv_sem=part_recv.at[kind, i, d],
            device_id=(rep, nexts[d], col),
            device_id_type=MESH,
        )

    def result_copy(kind, i, d):
        return pltpu.make_async_remote_copy(
            src_ref=result.at[kind, i, 1 - d],
            dst_ref=result.at[kind, i, 1 - d],
            send_sem=res_send.at[kind, i, d],
            recv_sem=res_recv.at[kind, i, d],
            device_id=(rep, nexts[d], col),
            device_id_type=MESH,
        )

    def out_copy(kind, i, h):
        target = (act_hbm, grad_hbm)[kind]
        return pltpu.make_async_copy(
            result.at[kind, i, h],
            target.at[:, pl.ds(pl.multiple_of(i * GROUP + h * HALF, HALF), HALF)],
            out_sem.at[kind, i, h],
        )

    def make_part(kind, i):
        if kind == 0:
            value = product(xa[...], w1[i])
        else:
            value = right_product(sa[...], w2[i])
        value = narrow(value)
        part[kind, i, 0] = value[:, :HALF]
        part[kind, i, 1] = value[:, HALF:]

    def finish(kind, i, d):
        total = wide(part[0, i, d]) + wide(came[0, i, d])
        if kind == 0:
            result[0, i, d] = narrow(gelu_tanh(total))
        else:
            slope = wide(part[1, i, d]) + wide(came[1, i, d])
            result[1, i, d] = narrow(slope * gelu_slope(total))

    def add_up(kind, i):
        left = jnp.concatenate([result[kind, i, 0], result[kind, i, 1]], axis=1)

        def strip(n):
            columns = rows_at(n * GROUP, GROUP)
            if kind == 0:
                more = product(left, w2[i, :, columns])
            else:
                more = right_product(left, w1[i, columns, :])

            @pl.when(i == 0)
            def _():
                acc[kind, :, columns] = more

            @pl.when(i > 0)
            def _():
                acc[kind, :, columns] = acc[kind, :, columns] + more

        each(width // GROUP, strip)

    def tick_part(kind, d, i):
        place = places[d]

        @pl.when(place > 0)
        def _():
            part_copy(kind, i, d).wait_recv()

        @pl.when(jnp.logical_and(place > 0, place < n_row - 1))
        def _():
            part[kind, i, d] = narrow(wide(part[kind, i, d]) + wide(came[kind, i, d]))

        @pl.when(place < n_row - 1)
        def _():
            part_copy(kind, i, d).start()

        @pl.when(place == n_row - 1)
        def _():
            finish(kind, i, d)

    def tick_result(kind, d, i):
        @pl.when(places[d] > 0)
        def _():
            result_copy(kind, i, d).wait_recv()

        @pl.when(places[d] < n_row - 1)
        def _():
            result_copy(kind, i, d).start()

    def pair2_copy(kind):
        return pltpu.make_async_remote_copy(
            src_ref=pair_out.at[kind],
            dst_ref=pair_in.at[kind],
            send_sem=pair2_send.at[kind],
            recv_sem=pair2_recv.at[kind],
            device_id=(partner, row, col),
            device_id_type=MESH,
        )

    def chip_copy(kind, k):
        chip_at, col_at = to_of(*offsets[k])
        return pltpu.make_async_remote_copy(
            src_ref=chip_out.at[kind, k],
            dst_ref=chip_in.at[kind, k],
            send_sem=chip_send.at[kind, k],
            recv_sem=chip_recv.at[kind, k],
            device_id=(2 * chip_at + core, row, col_at),
            device_id_type=MESH,
        )

    def sum_start(kind):
        for k in range(n_chip * n_col):
            rows = block_rows(k // n_col, 1 - core, k % n_col)
            pair_out[kind, k * tl:(k + 1) * tl, :] = narrow(acc[kind, rows, :])
        pair2_copy(kind).start()

    def both_cores(kind, chip_at, col_at):
        theirs = pair_in[kind, rows_at((chip_at * n_col + col_at) * tl, tl), :]
        return acc[kind, block_rows(chip_at, core, col_at), :] + wide(theirs)

    def sum_pass(kind):
        pair2_copy(kind).wait_recv()
        for k in range(near):
            chip_out[kind, k] = narrow(both_cores(kind, *to_of(*offsets[k])))
            chip_copy(kind, k).start()

    def sum_end(kind, target, base):
        total = both_cores(kind, chip, col)
        for k in range(near):
            chip_copy(kind, k).wait_recv()
            total = total + wide(chip_in[kind, k])
        target[...] = narrow(wide(base[...]) + total)

    def out_start(kind, i):
        for h in range(2):
            @pl.when(2 * i + h < halves)
            def _():
                out_copy(kind, i, h).start()

    xa_out = pltpu.make_async_copy(xa, xa_hbm, out_sem.at[0, groups, 0])
    sa_out = pltpu.make_async_copy(sa, sa_hbm, out_sem.at[0, groups, 1])

    for i in range(groups):
        w1_copy(i).wait()
    xa_out.start()
    make_part(0, 0)

    def tick(t):
        for d in range(2):
            m = t - places[d] * LAG
            for kind in range(kinds):
                i = m - kind * groups

                @pl.when(jnp.logical_and(i >= 0, i < groups))
                def _():
                    tick_part(kind, d, i)

            for kind in range(kinds):
                j = m - result_tick - kind * groups

                @pl.when(jnp.logical_and(j >= 0, j < groups))
                def _():
                    tick_result(kind, d, j)

        ahead = t + 1

        @pl.when(ahead < groups)
        def _():
            make_part(0, ahead)

        @pl.when(ahead == groups)
        def _():
            gather_end(1, scaled, sa)
            for i in range(groups):
                w2_copy(i).wait()
            sa_out.start()

        @pl.when(jnp.logical_and(ahead >= groups, ahead < 2 * groups))
        def _():
            make_part(1, ahead - groups)

        @pl.when(t == min(3, groups - 1))
        def _():
            gather_pass(1, scaled, sa)

        for kind in range(kinds):
            i = t - use_tick - kind * groups

            @pl.when(jnp.logical_and(i >= 0, i < groups))
            def _():
                out_start(kind, i)
                add_up(kind, i)

        @pl.when(t == use_tick + groups)
        def _():
            sum_start(0)

        @pl.when(t == use_tick + groups + 1)
        def _():
            sum_pass(0)

    each(ticks, tick)
    sum_start(1)
    sum_end(0, bo_ref, x_ref)
    sum_pass(1)
    sum_end(1, ig_ref, scaled)

    for which, source, target in ((0, x_ref, xa), (1, scaled, sa)):
        for k in range(near):
            near_copy(which, source, target, k).wait_send()
        for k in range(near + 1):
            pair_copy(which, source, target, k).wait_send()
    for kind in range(kinds):
        pair2_copy(kind).wait_send()
        for k in range(near):
            chip_copy(kind, k).wait_send()
    xa_out.wait()
    sa_out.wait()

    def drain(i):
        for kind in range(kinds):
            for d in range(2):
                @pl.when(places[d] < n_row - 1)
                def _():
                    part_copy(kind, i, d).wait_send()
                    result_copy(kind, i, d).wait_send()

                @pl.when(2 * i + d < halves)
                def _():
                    out_copy(kind, i, d).wait()

    each(groups, drain)


def weight_grad(left, right, strip):
    rows, depth = left.shape[1], left.shape[0]
    columns = right.shape[1]

    def kernel(left_ref, right_ref, out_ref):
        out_ref[...] = first_product(left_ref[...], right_ref[...])

    return pl.pallas_call(
        kernel,
        grid=(rows // strip,),
        in_specs=[
            pl.BlockSpec((depth, strip), lambda i: (0, i)),
            pl.BlockSpec((depth, columns), lambda i: (0, 0), pipeline_mode=pl.Buffered(1)),
        ],
        out_specs=pl.BlockSpec((strip, columns), lambda i: (i, 0)),
        out_shape=jax.ShapeDtypeStruct((rows, columns), jnp.float32),
        cost_estimate=pl.CostEstimate(
            flops=2 * rows * depth * columns,
            bytes_accessed=4 * rows * columns + 2 * depth * (rows + columns),
            transcendentals=0,
        ),
    )(left, right)


def strip_of(size):
    return 256 if size % 256 == 0 else 128


def body(inputs, w_in, w_out, cotangent, counts):
    tl, width = inputs.shape[1], inputs.shape[2]
    hidden = w_in.shape[1]
    n_rep, n_row, n_col = (lax.axis_size(name) for name in ("rep", "row", "col"))
    groups = -(-hidden // GROUP)
    rows = n_rep * n_col * tl
    blocks = n_rep * n_col // 2
    near = blocks - 1
    sizes = (n_rep, n_row, n_col, tl, width, hidden, groups)
    bf16, f32 = jnp.bfloat16, jnp.float32
    vmem = pl.BlockSpec(memory_space=pltpu.VMEM)
    anyw = pl.BlockSpec(memory_space=pl.ANY)
    dma = pltpu.SemaphoreType.DMA
    block_output, input_grad, activated, hidden_grad, tokens_all, scaled_all = pl.pallas_call(
        functools.partial(step_kernel, sizes),
        out_shape=(
            jax.ShapeDtypeStruct((tl, width), bf16),
            jax.ShapeDtypeStruct((tl, width), bf16),
            jax.ShapeDtypeStruct((rows, hidden), bf16),
            jax.ShapeDtypeStruct((rows, hidden), bf16),
            jax.ShapeDtypeStruct((rows, width), bf16),
            jax.ShapeDtypeStruct((rows, width), bf16),
        ),
        in_specs=[pl.BlockSpec(memory_space=pltpu.SMEM), vmem, vmem, anyw, anyw],
        out_specs=(vmem, vmem, anyw, anyw, anyw, anyw),
        scratch_shapes=[
            pltpu.VMEM((groups, width, GROUP), bf16),
            pltpu.VMEM((groups, GROUP, width), bf16),
            pltpu.VMEM((rows, width), bf16),
            pltpu.VMEM((rows, width), bf16),
            pltpu.VMEM((tl, width), bf16),
            pltpu.VMEM((2, groups, 2, rows, HALF), bf16),
            pltpu.VMEM((2, groups, 2, rows, HALF), bf16),
            pltpu.VMEM((2, groups, 2, rows, HALF), bf16),
            pltpu.VMEM((2, rows, width), f32),
            pltpu.VMEM((2, blocks * tl, width), bf16),
            pltpu.VMEM((2, blocks * tl, width), bf16),
            pltpu.VMEM((2, near, tl, width), bf16),
            pltpu.VMEM((2, near, tl, width), bf16),
            dma((2, groups)),
            dma((2, near)),
            dma((2, near)),
            dma((2, near + 1)),
            dma((2, near + 1)),
            dma((2, groups, 2)),
            dma((2, groups, 2)),
            dma((2, groups, 2)),
            dma((2, groups, 2)),
            dma((2, groups + 1, 2)),
            dma((2,)),
            dma((2,)),
            dma((2, near)),
            dma((2, near)),
        ],
        compiler_params=pltpu.CompilerParams(
            collective_id=0, has_side_effects=True, vmem_limit_bytes=67_000_000
        ),
    )(
        counts,
        inputs.reshape(tl, width),
        cotangent.reshape(tl, width),
        w_in,
        w_out,
    )
    w_out_grad = weight_grad(activated, scaled_all, strip_of(hidden))
    w_in_grad = weight_grad(tokens_all, hidden_grad, strip_of(width))
    return (
        block_output.reshape(1, tl, width),
        input_grad.reshape(1, tl, width),
        w_in_grad,
        w_out_grad,
    )


def solution(mesh):
    placed = (
        P("rep", "col", "row"),
        P("row", ("rep", "col")),
        P(("rep", "col"), "row"),
        P("rep", "col", "row"),
        P(),
    )
    return jax.shard_map(
        body,
        mesh=mesh,
        in_specs=placed,
        out_specs=(
            P("rep", "col", "row"),
            P("rep", "col", "row"),
            P("row", ("rep", "col")),
            P(("rep", "col"), "row"),
        ),
        check_vma=False,
    )
```

time: 390 us -> 210 us (0.54)
  waiting for transfers between devices: 267 us -> 0 us
  Pallas kernels: 0 us -> 208 us
  matrix products: 59.6 us -> 0 us
  local copies, waits for them, and re-layouts: 19.9 us -> 1.36 us
  between operations: 16.6 us -> 0.64 us
  other arithmetic: 15 us -> 0 us
  starting transfers between devices: 11.6 us -> 0 us
    pallas_call x0 -> x3, Pallas kernels: none -> 208 us  [the longest x1 183 us: body(): pl.pallas_call(functools.partial(step_kernel, sizes), out_shape=(jax.Shap...]
    reduce_scatter x2 -> x0, waiting for transfers between devices: 116 us -> none  [the longest x1 63 us: body(): lax.psum_scatter(partial_hidden.astype(jnp.bfloat16), 'row', scatter_dime...]
    all_gather x3 -> x0, waiting for transfers between devices: 115 us -> none  [the longest x1 62.5 us: body(): activated = lax.all_gather(active_share, 'row', axis=0, tiled=True)]
    dot_general x6 -> x0, matrix products: 59.6 us -> none  [the longest x2 20.9 us: first_product(): lax.dot_general(left, right, (((0,), (0,)), ((), ())), preferred_element_...]
    ppermute x9 -> x0, waiting for transfers between devices: 35.3 us -> none  [swapped(): return lax.ppermute(values, axis, pairs)]
    unnamed x13 -> x6, local copies, waits for them, and re-layouts: 19.9 us -> 1.36 us
    ppermute x9 -> x0, starting transfers between devices: 11.2 us -> none  [swapped(): return lax.ppermute(values, axis, pairs)]
    convert_element_type x7 -> x0, other arithmetic: 5.6 us -> none  [the longest x1 3.68 us: body(): grad_share = (slope_sum * gelu_slope(hidden)).astype(jnp.bfloat16)]
  transfers between devices with their start and end apart: 14 -> 0, of which waited for: 9 -> 0; matrix products, arithmetic and copies ran while one was open for 22% -> 0% of each run, Pallas kernels for 0% -> 0%
where the time goes in v1:
time: 210 us
  Pallas kernels  208 us (99%)
    pallas_call x1, Pallas kernels, body(): pl.pallas_call(functools.partial(step_kernel, sizes), out_shape=(jax.Shap...  183 us
    pallas_call x2, Pallas kernels, weight_grad(): pl.pallas_call(kernel, grid=(rows // strip,), in_specs=[pl.BlockSpec((dep...  24.8 us

profile of v1, /device:TPU:0, one launch (start us, length us, event | category | flops | bytes accessed | tf_op | source)
XLA Modules:
  0.0 209.7 jit_solution(1686075599061707653)
XLA Ops:
  0.6 182.8 %shard_map.84 = (bf16[64,1536]{1,0:T(8,128)(2,1)}, bf16[64,1536]{1,0:T(8,128)(2,1)}, bf16[512,3072]{1,0:T(8,128)(2,1)}, bf16[512,3072]{1,0:T(8,128)(2,1)}, bf16[...) custom-call(s32[4]{0:T(128)} %counts.1, bf16[64,1536]{1,0:T(8,128)(2,1)} %bitcast.4, bf16[64,1536]{1,0:T(8,128)(2,1)} %bitcast.5, ...), custom_call_target="tpu_custom_call" | custom-call | tf_op jit(solution)/shard_map/pallas_call | solution.py:483
  183.5 11.2 %shard_map.85 = f32[1536,3072]{1,0:T(8,128)} custom-call(bf16[512,1536]{1,0:T(8,128)(2,1)} %get-tuple-element.12.left_ref, bf16[512,3072]{1,0:T(8,128)(2,1)} %get-tuple-element.13.right_ref), custom_call_target="tpu_custom_call" | custom-call | flops 4831838208 | bytes 23592960 | tf_op jit(solution)/shard_map/pallas_call | solution.py:449
  194.6 0.0 copy-start.1
  194.6 0.0 copy-start
  194.6 13.7 %shard_map.86 = f32[3072,1536]{1,0:T(8,128)} custom-call(bf16[512,3072]{1,0:T(8,128)(2,1)} %get-tuple-element.14.left_ref, bf16[512,1536]{1,0:T(8,128)(2,1)} %get-tuple-element.15.right_ref), custom_call_target="tpu_custom_call" | custom-call | flops 4831838208 | bytes 23592960 | tf_op jit(solution)/shard_map/pallas_call | solution.py:449
  208.3 0.0 copy-done.1
  208.3 0.7 copy.11
  209.0 0.0 copy-done
  209.0 0.7 copy.12
Async XLA Ops:
  194.6 13.7 %copy-start.1 = (bf16[64,1536]{1,0:T(8,128)(2,1)S(1)}, bf16[64,1536]{1,0:T(8,128)(2,1)}, u32[]{:S(2)}) copy-start(bf16[64,1536]{1,0:T(8,128)(2,1)} %get-tuple-element.10) | copy-start | bytes 589828
  194.6 14.4 %copy-start = (bf16[64,1536]{1,0:T(8,128)(2,1)S(1)}, bf16[64,1536]{1,0:T(8,128)(2,1)}, u32[]{:S(2)}) copy-start(bf16[64,1536]{1,0:T(8,128)(2,1)} %get-tuple-element.11) | copy-start | bytes 589828

commit v2 on v1

v2 whole, which is shorter than its diff:
```python
import functools

import jax
import jax.numpy as jnp
from jax import lax
from jax.experimental import pallas as pl
from jax.experimental.pallas import tpu as pltpu
from jax.sharding import PartitionSpec as P

MBT = 32
HALF = 128
GROUP = 2 * HALF
LAG = 3
SLOTS = 3
EIGHTHS = (4, 5, 6, 8)
MESH = pl.DeviceIdType.MESH

root_coef = 0.7978845608028654
cubic_coef = 0.044715


def gelu_tanh(values):
    inner = root_coef * (values + cubic_coef * values * values * values)
    return 0.5 * values * (1.0 + jnp.tanh(inner))


def gelu_slope(values):
    inner = root_coef * (values + cubic_coef * values * values * values)
    tangent = jnp.tanh(inner)
    return 0.5 * (1.0 + tangent) + 0.5 * values * (1.0 - tangent * tangent) * root_coef * (
        1.0 + 3.0 * cubic_coef * values * values
    )


def wide(values):
    return values.astype(jnp.float32)


def narrow(values):
    return values.astype(jnp.bfloat16)


def product(left, right):
    return jnp.dot(left, right, preferred_element_type=jnp.float32)


def right_product(left, right):
    return lax.dot_general(
        left, right, (((1,), (1,)), ((), ())), preferred_element_type=jnp.float32
    )


def first_product(left, right):
    return lax.dot_general(
        left, right, (((0,), (0,)), ((), ())), preferred_element_type=jnp.float32
    )


def rows_at(start, size):
    return pl.ds(pl.multiple_of(start, size), size)


def each(count, body):
    lax.fori_loop(0, count, lambda i, c: (body(i), c)[1], 0)


def distances(n_chip, n_col):
    return [(i, j) for i in range(n_chip) for j in range(n_col) if i + j > 0]


def step_kernel(
    sizes,
    counts, x_ref, cot_ref, w1_hbm, w2_hbm,
    bo_ref, act_hbm, grad_hbm, xk_hbm, sk_hbm, base_ref, *others,
):
    n_rep, n_row, n_col, tl, width, hidden, groups, rows, kept_rows = sizes
    near = n_rep * n_col // 2 - 1
    sent_refs, scratch = others[:near], others[near:]
    (
    w1, w2, xa, sa, scaled, xk, sk, picked, placed, back,
    part_h, part_s, came_h, came_s, result_h, result_s, packed,
    acc_h, acc_s, pair_out, pair_in, chip_out, chip_in,
    w_sem, near_send, near_recv, pair_send, pair_recv,
    part_send, part_recv, res_send, res_recv, out_sem,
    pair2_send, pair2_recv, chip_send, chip_recv,
    ) = scratch
    halves = hidden // HALF
    pack = kept_rows < rows
    unit = min(tl, MBT)
    per_block = tl // unit
    rep, row, col = (lax.axis_index(name) for name in ("rep", "row", "col"))
    core, chip = lax.rem(rep, 2), rep // 2
    n_chip = n_rep // 2
    partner = rep + 1 - 2 * core
    offsets = distances(n_chip, n_col)
    part, came = (part_h, part_s), (came_h, came_s)
    result, acc = (result_h, result_s), (acc_h, acc_s)

    def to_of(k):
        i, j = offsets[k]
        return lax.rem(chip + i, n_chip), lax.rem(col + j, n_col)

    def from_of(k):
        i, j = offsets[k]
        return lax.rem(chip + n_chip - i, n_chip), lax.rem(col + n_col - j, n_col)

    def block_to(k):
        i, j = offsets[k]
        return 1 + offsets.index(((n_chip - i) % n_chip, (n_col - j) % n_col))

    def block_rows(j, core_at):
        return rows_at((2 * j + core_at) * tl, tl)

    def size_of(i):
        return min(GROUP, hidden - i * GROUP)

    def w1_copy(i):
        return pltpu.make_async_copy(
            w1_hbm.at[:, pl.ds(i * GROUP, size_of(i))],
            w1.at[i, :, pl.ds(0, size_of(i))],
            w_sem.at[0, i],
        )

    def w2_copy(i):
        return pltpu.make_async_copy(
            w2_hbm.at[pl.ds(i * GROUP, size_of(i)), :],
            w2.at[i, pl.ds(0, size_of(i)), :],
            w_sem.at[1, i],
        )

    for i in range(groups):
        if size_of(i) < GROUP:
            w1[i, :, size_of(i):] = jnp.zeros((width, GROUP - size_of(i)), jnp.bfloat16)
            w2[i, size_of(i):, :] = jnp.zeros((GROUP - size_of(i), width), jnp.bfloat16)
        w1_copy(i).start()
    for i in range(groups):
        w2_copy(i).start()

    barrier = pltpu.get_barrier_semaphore()
    for k in range(near):
        chip_at, col_at = to_of(k)
        pl.semaphore_signal(
            barrier, inc=1, device_id=(2 * chip_at + core, row, col_at), device_id_type=MESH
        )
    pl.semaphore_signal(barrier, inc=1, device_id=(partner, row, col), device_id_type=MESH)

    @pl.when(row > 0)
    def _():
        pl.semaphore_signal(barrier, inc=1, device_id=(rep, row - 1, col), device_id_type=MESH)

    @pl.when(row < n_row - 1)
    def _():
        pl.semaphore_signal(barrier, inc=1, device_id=(rep, row + 1, col), device_id_type=MESH)

    at_ends = jnp.where(row > 0, 1, 0) + jnp.where(row < n_row - 1, 1, 0)
    pl.semaphore_wait(barrier, near + 1 + at_ends)

    def near_copy(which, source, target, k):
        chip_at, col_at = to_of(k)
        return pltpu.make_async_remote_copy(
            src_ref=source,
            dst_ref=target.at[block_rows(k + 1, core), :],
            send_sem=near_send.at[which, k],
            recv_sem=near_recv.at[which, k],
            device_id=(2 * chip_at + core, row, col_at),
            device_id_type=MESH,
        )

    def pair_copy(which, source, target, j):
        there = target.at[block_rows(j, core), :]
        return pltpu.make_async_remote_copy(
            src_ref=source if j == 0 else there,
            dst_ref=there,
            send_sem=pair_send.at[which, j],
            recv_sem=pair_recv.at[which, j],
            device_id=(partner, row, col),
            device_id_type=MESH,
        )

    def gather_start(which, source, target):
        pair_copy(which, source, target, 0).start()
        for k in range(near):
            near_copy(which, source, target, k).start()

    def gather_pass(which, source, target):
        for k in range(near):
            near_copy(which, source, target, k).wait_recv()
            pair_copy(which, source, target, k + 1).start()

    def gather_end(which, source, target):
        for j in range(1, near + 1):
            pair_copy(which, source, target, j).wait_recv()

    gather_start(0, x_ref, xa)
    xa[block_rows(0, core), :] = x_ref[...]
    counted = counts[0]
    for r in range(1, n_rep):
        counted = counted + counts[r]
    token_total = (MBT * counted).astype(jnp.float32)
    position = col * tl + lax.broadcasted_iota(jnp.int32, (tl, width), 0)
    kept = jnp.where(position < MBT * counts[rep], 1.0, 0.0)
    value = narrow(wide(cot_ref[...]) * kept / token_total)
    scaled[...] = value
    sa[block_rows(0, core), :] = value

    def place_units():
        flags = []
        for j in range(near + 1):
            chip_at, col_at = (chip, col) if j == 0 else from_of(j - 1)
            for core_at in range(2):
                for u in range(per_block):
                    batch = (col_at * tl + u * unit) // MBT
                    flags.append(jnp.where(batch < counts[2 * chip_at + core_at], 1, 0))
        total = flags[0]
        for flag in flags[1:]:
            total = total + flag
        before = 0 * total
        row_of = lax.broadcasted_iota(jnp.int32, (kept_rows, rows), 0)
        at_of = lax.broadcasted_iota(jnp.int32, (1, rows), 1)
        target = 0 * at_of
        kept_at = lax.broadcasted_iota(jnp.int32, (unit, kept_rows), 1)
        unit_at = lax.broadcasted_iota(jnp.int32, (unit, kept_rows), 0)
        for at, flag in enumerate(flags):
            first = unit * jnp.where(flag > 0, before, total + at - before)
            before = before + flag
            inside = jnp.logical_and(at_of >= at * unit, at_of < (at + 1) * unit)
            target = jnp.where(inside, first + at_of - at * unit, target)
            placed[at * unit:(at + 1) * unit, :] = narrow(
                jnp.where(kept_at == unit_at + first, 1.0, 0.0)
            )
        picked[...] = narrow(jnp.where(row_of == target, 1.0, 0.0))

    if pack:
        place_units()

    def kept_of(source, target):
        def strip(n):
            columns = rows_at(n * GROUP, GROUP)
            target[:, columns] = narrow(product(picked[...], source[:, columns]))

        each(width // GROUP, strip)

    places = (row, n_row - 1 - row)
    nexts = (row + 1, row - 1)
    furthest = jnp.maximum(row, n_row - 1 - row)
    part_runs = ((0, 0, 2 * tl), (0, 2 * tl, rows), (1, 0, kept_rows))
    result_runs = ((0, 0, rows), (1, 0, kept_rows))
    result_tick = max(len(part_runs) * groups, (n_row - 1) * LAG + 1 + groups)
    use_tick = result_tick + (n_row - 1) * LAG
    ticks = use_tick + len(result_runs) * groups

    def part_copy(run, i, d):
        kind, low, high = part_runs[run]
        return pltpu.make_async_remote_copy(
            src_ref=part[kind].at[i, d, pl.ds(low, high - low), :],
            dst_ref=came[kind].at[i, d, pl.ds(low, high - low), :],
            send_sem=part_send.at[run, i, d],
            recv_sem=part_recv.at[run, i, d],
            device_id=(rep, nexts[d], col),
            device_id_type=MESH,
        )

    def result_copy(run, i, d):
        kind, low, high = result_runs[run]
        there = result[kind].at[i, 1 - d, pl.ds(low, high - low), :]
        return pltpu.make_async_remote_copy(
            src_ref=there,
            dst_ref=there,
            send_sem=res_send.at[run, i, d],
            recv_sem=res_recv.at[run, i, d],
            device_id=(rep, nexts[d], col),
            device_id_type=MESH,
        )

    def out_copy(kind, i, h):
        source = result_s if kind == 1 else packed if pack else result_h
        target = (act_hbm, grad_hbm)[kind]
        return pltpu.make_async_copy(
            source.at[i, h],
            target.at[:, pl.ds(pl.multiple_of(i * GROUP + h * HALF, HALF), HALF)],
            out_sem.at[kind, i, h],
        )

    def make_part(run, i):
        kind, low, high = part_runs[run]
        if kind == 0:
            value = product(xa[low:high, :], w1[i])
        else:
            value = right_product(sk[...], w2[i])
        value = narrow(value)
        part[kind][i, 0, low:high, :] = value[:, :HALF]
        part[kind][i, 1, low:high, :] = value[:, HALF:]

    def finish(run, i, d):
        kind, low, high = part_runs[run]
        if kind == 0:
            total = wide(part_h[i, d, low:high, :]) + wide(came_h[i, d, low:high, :])
            result_h[i, d, low:high, :] = narrow(gelu_tanh(total))
        elif not pack:
            total = wide(part_h[i, d]) + wide(came_h[i, d])
            slope = wide(part_s[i, d]) + wide(came_s[i, d])
            result_s[i, d] = narrow(slope * gelu_slope(total))
        else:
            total = product(picked[...], part_h[i, d]) + product(picked[...], came_h[i, d])
            slope = wide(part_s[i, d]) + wide(came_s[i, d])
            result_s[i, d] = narrow(slope * gelu_slope(total))

    def add_up(kind, i):
        left = jnp.concatenate([result[kind][i, 0], result[kind][i, 1]], axis=1)

        def strip(n):
            columns = rows_at(n * GROUP, GROUP)
            if kind == 0:
                more = product(left, w2[i, :, columns])
            else:
                more = right_product(left, w1[i, columns, :])

            @pl.when(i == 0)
            def _():
                acc[kind][:, columns] = more

            @pl.when(i > 0)
            def _():
                acc[kind][:, columns] = acc[kind][:, columns] + more

        each(width // GROUP, strip)

    def tick_part(run, d, i):
        kind, low, high = part_runs[run]
        place = places[d]

        @pl.when(place > 0)
        def _():
            part_copy(run, i, d).wait_recv()

        @pl.when(jnp.logical_and(place > 0, place < n_row - 1))
        def _():
            part[kind][i, d, low:high, :] = narrow(
                wide(part[kind][i, d, low:high, :]) + wide(came[kind][i, d, low:high, :])
            )

        @pl.when(place < n_row - 1)
        def _():
            part_copy(run, i, d).start()

        @pl.when(place == n_row - 1)
        def _():
            finish(run, i, d)

    def tick_result(run, d, i):
        @pl.when(places[d] > 0)
        def _():
            result_copy(run, i, d).wait_recv()

        @pl.when(places[d] < n_row - 1)
        def _():
            result_copy(run, i, d).start()

    def acc_rows(kind, j, core_at):
        if kind == 0 or not pack:
            return acc[kind][block_rows(j, core_at), :]
        return wide(back[block_rows(j, core_at), :])

    def unpack():
        def strip(n):
            columns = rows_at(n * GROUP, GROUP)
            back[:, columns] = narrow(product(placed[...], narrow(acc_s[:, columns])))

        each(width // GROUP, strip)

    def pair2_copy(kind):
        return pltpu.make_async_remote_copy(
            src_ref=pair_out.at[kind],
            dst_ref=pair_in.at[kind],
            send_sem=pair2_send.at[kind],
            recv_sem=pair2_recv.at[kind],
            device_id=(partner, row, col),
            device_id_type=MESH,
        )

    def chip_copy(k):
        chip_at, col_at = to_of(k)
        return pltpu.make_async_remote_copy(
            src_ref=chip_out.at[k],
            dst_ref=chip_in.at[k],
            send_sem=chip_send.at[k],
            recv_sem=chip_recv.at[k],
            device_id=(2 * chip_at + core, row, col_at),
            device_id_type=MESH,
        )

    def sum_start(kind):
        for j in range(near + 1):
            pair_out[kind, j * tl:(j + 1) * tl, :] = narrow(acc_rows(kind, j, 1 - core))
        pair2_copy(kind).start()

    def both_cores(kind, j):
        return acc_rows(kind, j, core) + wide(pair_in[kind, j * tl:(j + 1) * tl, :])

    def sum_pass():
        pair2_copy(0).wait_recv()
        for k in range(near):
            chip_out[k] = narrow(both_cores(0, block_to(k)))
            chip_copy(k).start()

    def sum_end():
        total = both_cores(0, 0)
        for k in range(near):
            chip_copy(k).wait_recv()
            total = total + wide(chip_in[k])
        bo_ref[...] = narrow(wide(x_ref[...]) + total)

    def out_start(kind, i):
        for h in range(2):
            @pl.when(2 * i + h < halves)
            def _():
                out_copy(kind, i, h).start()

    def pack_result(i):
        both = jnp.concatenate([result_h[i, 0], result_h[i, 1]], axis=1)
        both = narrow(product(picked[...], both))
        packed[i, 0] = both[:, :HALF]
        packed[i, 1] = both[:, HALF:]

    x_kept, s_kept = (xk, sk) if pack else (xa, sa)
    xk_out = pltpu.make_async_copy(x_kept, xk_hbm, out_sem.at[0, groups, 0])
    sk_out = pltpu.make_async_copy(s_kept, sk_hbm, out_sem.at[0, groups, 1])
    if not pack:
        sk = sa

    for i in range(groups):
        w1_copy(i).wait()
    pair_copy(0, x_ref, xa, 0).wait_recv()
    make_part(0, 0)

    def tick(t):
        for d in range(2):
            m = t - places[d] * LAG
            for run in range(len(part_runs)):
                i = m - run * groups

                @pl.when(jnp.logical_and(i >= 0, i < groups))
                def _():
                    tick_part(run, d, i)

            for run in range(len(result_runs)):
                i = m - result_tick - run * groups

                @pl.when(jnp.logical_and(i >= 0, i < groups))
                def _():
                    tick_result(run, d, i)

        @pl.when(t == max(0, groups - 4))
        def _():
            gather_pass(0, x_ref, xa)
            gather_start(1, scaled, sa)

        @pl.when(t == groups - 1)
        def _():
            gather_end(0, x_ref, xa)

        @pl.when(t == groups)
        def _():
            if pack:
                kept_of(xa, xk)
            xk_out.start()

        @pl.when(t == groups + groups // 2)
        def _():
            gather_pass(1, scaled, sa)

        @pl.when(t == 2 * groups - 1)
        def _():
            pair_copy(1, scaled, sa, 0).wait_recv()
            gather_end(1, scaled, sa)
            if pack:
                kept_of(sa, sk)
            for i in range(groups):
                w2_copy(i).wait()
            sk_out.start()

        for run in range(len(part_runs)):
            i = t + 1 - run * groups

            @pl.when(jnp.logical_and(i >= 0, i < groups))
            def _():
                make_part(run, i)

        for kind in range(2):
            i = t - result_tick - furthest * LAG - kind * groups

            @pl.when(jnp.logical_and(i >= 0, i < groups))
            def _():
                add_up(kind, i)
                if kind == 1:
                    out_start(1, i)
                    if pack:
                        pack_result(i)
                    out_start(0, i)

        @pl.when(t == use_tick + groups)
        def _():
            sum_start(0)

        @pl.when(t == use_tick + groups + 1)
        def _():
            sum_pass()

    each(ticks, tick)
    if pack:
        unpack()
    sum_start(1)
    sum_end()
    pair2_copy(1).wait_recv()
    base_ref[...] = wide(scaled[...]) + both_cores(1, 0)
    for k in range(near):
        sent_refs[k][...] = narrow(both_cores(1, block_to(k)))

    for which, source, target in ((0, x_ref, xa), (1, scaled, sa)):
        for k in range(near):
            near_copy(which, source, target, k).wait_send()
        for j in range(near + 1):
            pair_copy(which, source, target, j).wait_send()
    for kind in range(2):
        pair2_copy(kind).wait_send()
    for k in range(near):
        chip_copy(k).wait_send()
    xk_out.wait()
    sk_out.wait()

    def drain(i):
        for d in range(2):
            @pl.when(places[d] < n_row - 1)
            def _():
                for run in range(len(part_runs)):
                    part_copy(run, i, d).wait_send()
                for run in range(len(result_runs)):
                    result_copy(run, i, d).wait_send()

            for kind in range(2):
                @pl.when(2 * i + d < halves)
                def _():
                    out_copy(kind, i, d).wait()

    each(groups, drain)


def strip_of(size, most):
    return next(strip for strip in (512, 256, 128) if strip <= most and size % strip == 0)


def weight_grads(activated, scaled, tokens, hidden_grad, block_output):
    depth, hidden = activated.shape
    width = scaled.shape[1]
    high, low = strip_of(hidden, 512), strip_of(width, 512)
    cuts = 2 if hidden % (2 * HALF) == 0 else 1
    across = hidden // cuts
    first_jobs, second_jobs = hidden // high, width // low * cuts

    def kernel(
        a_hbm, s_hbm, x_hbm, g_hbm, b_hbm, out_grad, in_grad, b_out,
        a, s, x, g, b, first_slots, second_slots, in_sem, first_sem, second_sem, b_sem,
    ):
        def a_copy(i):
            columns = rows_at(i * high, high)
            return pltpu.make_async_copy(a_hbm.at[:, columns], a.at[:, columns], in_sem.at[3 + i])

        def first_out(i):
            slot = lax.rem(i, SLOTS)
            return pltpu.make_async_copy(
                first_slots.at[slot], out_grad.at[rows_at(i * high, high), :], first_sem.at[slot]
            )

        def second_out(i):
            slot = lax.rem(i, SLOTS)
            rows, columns = rows_at(i // cuts * low, low), rows_at(lax.rem(i, cuts) * across, across)
            return pltpu.make_async_copy(
                second_slots.at[slot], in_grad.at[rows, columns], second_sem.at[slot]
            )

        s_copy = pltpu.make_async_copy(s_hbm, s, in_sem.at[0])
        x_copy = pltpu.make_async_copy(x_hbm, x, in_sem.at[1])
        g_copy = pltpu.make_async_copy(g_hbm, g, in_sem.at[2])
        b_copy = pltpu.make_async_copy(b_hbm, b, b_sem.at[0])
        b_back = pltpu.make_async_copy(b, b_out, b_sem.at[1])
        s_copy.start()
        for i in range(first_jobs):
            a_copy(i).start()
        x_copy.start()
        g_copy.start()
        b_copy.start()
        s_copy.wait()

        def first(i):
            a_copy(i).wait()

            @pl.when(i >= SLOTS)
            def _():
                first_out(i - SLOTS).wait()

            left = a[:, rows_at(i * high, high)]
            first_slots[lax.rem(i, SLOTS)] = first_product(left, s[...])
            first_out(i).start()

        each(first_jobs, first)
        x_copy.wait()
        g_copy.wait()
        b_copy.wait()
        b_back.start()

        def second(i):
            @pl.when(i >= SLOTS)
            def _():
                second_out(i - SLOTS).wait()

            left = x[:, rows_at(i // cuts * low, low)]
            right = g[:, rows_at(lax.rem(i, cuts) * across, across)]
            second_slots[lax.rem(i, SLOTS)] = first_product(left, right)
            second_out(i).start()

        each(second_jobs, second)
        for i in range(max(0, first_jobs - SLOTS), first_jobs):
            first_out(i).wait()
        for i in range(max(0, second_jobs - SLOTS), second_jobs):
            second_out(i).wait()
        b_back.wait()

    anyw = pl.BlockSpec(memory_space=pl.ANY)
    bf16, f32 = jnp.bfloat16, jnp.float32
    return pl.pallas_call(
        kernel,
        in_specs=[anyw] * 5,
        out_specs=(anyw,) * 3,
        out_shape=(
            jax.ShapeDtypeStruct((hidden, width), f32),
            jax.ShapeDtypeStruct((width, hidden), f32),
            jax.ShapeDtypeStruct(block_output.shape, bf16),
        ),
        scratch_shapes=[
            pltpu.VMEM((depth, hidden), bf16),
            pltpu.VMEM((depth, width), bf16),
            pltpu.VMEM((depth, width), bf16),
            pltpu.VMEM((depth, hidden), bf16),
            pltpu.VMEM(block_output.shape, bf16),
            pltpu.VMEM((SLOTS, high, width), f32),
            pltpu.VMEM((SLOTS, low, across), f32),
            pltpu.SemaphoreType.DMA((3 + first_jobs,)),
            pltpu.SemaphoreType.DMA((SLOTS,)),
            pltpu.SemaphoreType.DMA((SLOTS,)),
            pltpu.SemaphoreType.DMA((2,)),
        ],
        compiler_params=pltpu.CompilerParams(vmem_limit_bytes=60_000_000),
        cost_estimate=pl.CostEstimate(
            flops=4 * hidden * depth * width,
            bytes_accessed=8 * hidden * width + 4 * depth * (hidden + width),
            transcendentals=0,
        ),
    )(activated, scaled, tokens, hidden_grad, block_output)


def step(sizes, number, counts, inputs, cotangent, w_in, w_out):
    n_rep, n_row, n_col, tl, width, hidden, groups, rows, kept_rows = sizes
    blocks = n_rep * n_col // 2
    near = blocks - 1
    pack = kept_rows < rows
    spare = kept_rows if pack else 16
    bf16, f32 = jnp.bfloat16, jnp.float32
    vmem = pl.BlockSpec(memory_space=pltpu.VMEM)
    anyw = pl.BlockSpec(memory_space=pl.ANY)
    dma = pltpu.SemaphoreType.DMA
    block_output, activated, hidden_grad, tokens_kept, scaled_kept, base, *sent = pl.pallas_call(
        functools.partial(step_kernel, sizes),
        out_shape=(
            jax.ShapeDtypeStruct((tl, width), bf16),
            jax.ShapeDtypeStruct((kept_rows, hidden), bf16),
            jax.ShapeDtypeStruct((kept_rows, hidden), bf16),
            jax.ShapeDtypeStruct((kept_rows, width), bf16),
            jax.ShapeDtypeStruct((kept_rows, width), bf16),
            jax.ShapeDtypeStruct((tl, width), f32),
            *[jax.ShapeDtypeStruct((tl, width), bf16)] * near,
        ),
        in_specs=[pl.BlockSpec(memory_space=pltpu.SMEM), vmem, vmem, anyw, anyw],
        out_specs=(vmem, anyw, anyw, anyw, anyw, vmem, *[vmem] * near),
        scratch_shapes=[
            pltpu.VMEM((groups, width, GROUP), bf16),
            pltpu.VMEM((groups, GROUP, width), bf16),
            pltpu.VMEM((rows, width), bf16),
            pltpu.VMEM((rows, width), bf16),
            pltpu.VMEM((tl, width), bf16),
            pltpu.VMEM((spare, width), bf16),
            pltpu.VMEM((spare, width), bf16),
            pltpu.VMEM((spare, rows), bf16),
            pltpu.VMEM((rows, spare), bf16),
            pltpu.VMEM((rows if pack else 16, width), bf16),
            pltpu.VMEM((groups, 2, rows, HALF), bf16),
            pltpu.VMEM((groups, 2, kept_rows, HALF), bf16),
            pltpu.VMEM((groups, 2, rows, HALF), bf16),
            pltpu.VMEM((groups, 2, kept_rows, HALF), bf16),
            pltpu.VMEM((groups, 2, rows, HALF), bf16),
            pltpu.VMEM((groups, 2, kept_rows, HALF), bf16),
            pltpu.VMEM((groups, 2, spare, HALF), bf16),
            pltpu.VMEM((rows, width), f32),
            pltpu.VMEM((kept_rows, width), f32),
            pltpu.VMEM((2, blocks * tl, width), bf16),
            pltpu.VMEM((2, blocks * tl, width), bf16),
            pltpu.VMEM((near, tl, width), bf16),
            pltpu.VMEM((near, tl, width), bf16),
            dma((2, groups)),
            dma((2, near)),
            dma((2, near)),
            dma((2, near + 1)),
            dma((2, near + 1)),
            dma((3, groups, 2)),
            dma((3, groups, 2)),
            dma((2, groups, 2)),
            dma((2, groups, 2)),
            dma((2, groups + 1, 2)),
            dma((2,)),
            dma((2,)),
            dma((near,)),
            dma((near,)),
        ],
        compiler_params=pltpu.CompilerParams(
            collective_id=number, has_side_effects=True, vmem_limit_bytes=67_000_000
        ),
    )(counts, inputs, cotangent, w_in, w_out)
    n_chip = n_rep // 2
    total = base
    for (i, j), own in zip(distances(n_chip, n_col), sent):
        pairs = [
            (
                (2 * chip + core) * n_col + col,
                (2 * ((chip + i) % n_chip) + core) * n_col + (col + j) % n_col,
            )
            for chip in range(n_chip) for core in range(2) for col in range(n_col)
        ]
        total = total + wide(lax.ppermute(own, ("rep", "col"), pairs))
    w_out_grad, w_in_grad, block_output = weight_grads(
        activated, scaled_kept, tokens_kept, hidden_grad, block_output
    )
    return block_output, narrow(total), w_in_grad, w_out_grad


def body(inputs, w_in, w_out, cotangent, counts):
    tl, width = inputs.shape[1], inputs.shape[2]
    hidden = w_in.shape[1]
    n_rep, n_row, n_col = (lax.axis_size(name) for name in ("rep", "row", "col"))
    rows = n_rep * n_col * tl
    cases = [rows * eighths // 8 for eighths in EIGHTHS]
    sizes = (n_rep, n_row, n_col, tl, width, hidden, -(-hidden // GROUP), rows)
    kept_rows = MBT * jnp.sum(counts)
    case = sum((kept_rows > rows_of_case).astype(jnp.int32) for rows_of_case in cases[:-1])
    args = (
        counts, inputs.reshape(tl, width), cotangent.reshape(tl, width), w_in, w_out
    )
    branches = [
        functools.partial(step, (*sizes, kept), number) for number, kept in enumerate(cases)
    ]
    if len(branches) == 1:
        block_output, input_grad, w_in_grad, w_out_grad = branches[0](*args)
    else:
        block_output, input_grad, w_in_grad, w_out_grad = lax.switch(case, branches, *args)
    return (
        block_output.reshape(1, tl, width),
        input_grad.reshape(1, tl, width),
        w_in_grad,
        w_out_grad,
    )


def solution(mesh):
    placed = (
        P("rep", "col", "row"),
        P("row", ("rep", "col")),
        P(("rep", "col"), "row"),
        P("rep", "col", "row"),
        P(),
    )
    return jax.shard_map(
        body,
        mesh=mesh,
        in_specs=placed,
        out_specs=(
            P("rep", "col", "row"),
            P("rep", "col", "row"),
            P("row", ("rep", "col")),
            P(("rep", "col"), "row"),
        ),
        check_vma=False,
    )
```

time: 210 us -> 178 us (0.85); the launches traced: 210 us -> 175 us
  Pallas kernels: 208 us -> 167 us
  starting transfers between devices: 0 us -> 3.55 us
    pallas_call x3 -> x2, Pallas kernels: 208 us -> 167 us  [the longest x1 152 us: step(): pl.pallas_call(functools.partial(step_kernel, sizes), out_shape=(jax.Shap...]
    ppermute x0 -> x3, starting transfers between devices: none -> 3.55 us  [step(): total = total + wide(lax.ppermute(own, ('rep', 'col'), pairs))]
  transfers between devices with their start and end apart: 0 -> 3, of which waited for: 0 -> 0; matrix products, arithmetic and copies ran while one was open for 0% -> 0% of each run, Pallas kernels for 0% -> 9%
where the time goes in v2:
time: 178 us; the launch traced here: 175 us
  Pallas kernels  167 us (94%)
  starting transfers between devices  3.55 us (2%)
    pallas_call x1, Pallas kernels, step(): pl.pallas_call(functools.partial(step_kernel, sizes), out_shape=(jax.Shap...  152 us
    pallas_call x1, Pallas kernels, weight_grads(): pl.pallas_call(kernel, in_specs=[anyw] * 5, out_specs=(anyw,) * 3, out_sh...  15.4 us
  transfers between devices with their start and end apart: 3, of which 0 were waited for; matrix products, arithmetic and copies ran while one was open for 0% of the time, Pallas kernels for 9%

profile of v2, /device:TPU:0, one launch (start us, length us, event | category | flops | bytes accessed | tf_op | source)
XLA Modules:
  0.0 175.0 jit_solution(1233996328850140981)
XLA Ops:
  0.6 1.3 reduce_sum.9
  2.6 171.7 %conditional.1 = (bf16[64,1536]{1,0:T(8,128)(2,1)}, f32[1536,3072]{1,0:T(8,128)}, f32[3072,1536]{1,0:T(8,128)}, bf16[1,64,1536]{2,1,0:T(8,128)(2,1)S(1)}) conditional(s32[]{:T(128)} %clamp.3, (s32[4]{0:T(128)}, bf16[64,1536]{1,0:T(8,128)(2,1)}, bf16[64,1536]{1,0:T(8,128)(2,1)}, bf16[1536,3072]{1,0:T(8,128)(2,1)}, ...), branch_computations={%region_1.0_spmd, %region_2.0_spmd, %region_3.0_spmd, %region_4.0_... | conditional | flops 9664364544 | bytes 52297908 | solution.py:762
  2.6 152.1 %branch_1_fun.2 = (bf16[64,1536]{1,0:T(8,128)(2,1)}, bf16[320,3072]{1,0:T(8,128)(2,1)}, bf16[320,3072]{1,0:T(8,128)(2,1)}, bf16[320,1536]{1,0:T(8,128)(2,1)}, bf...) custom-call(s32[4]{0:T(128)} %get-tuple-element.58.counts, ...), custom_call_target="tpu_custom_call" | custom-call | tf_op jit(solution)/shard_map/cond/branch_1_fun/pallas_call | solution.py:671
  154.7 1.3 collective-permute-start.3
  156.0 1.5 collective-permute-start.4
  157.5 0.7 collective-permute-start.5
  158.3 0.0 copy-start.1
  158.3 15.4 %branch_1_fun.3 = (f32[3072,1536]{1,0:T(8,128)}, f32[1536,3072]{1,0:T(8,128)}, bf16[64,1536]{1,0:T(8,128)(2,1)}) custom-call(bf16[320,3072]{1,0:T(8,128)(2,1)} %get-tuple-element.63.a_hbm, bf16[320,1536]{1,0:T(8,128)(2,1)} %get-tuple-element.64.s_hbm, bf16[320,1536]{1,0:T(8,128)(2,1)} %get-tuple-element.65.x_hbm, bf16[320,3072]{1,0:T(8,128)(2,1)} %get-tuple-element.66.g_hbm, ...), custom_call_target="tpu_custom_call" | custom-call | flops 6039797760 | bytes 43646976 | tf_op jit(solution)/shard_map/cond/branch_1_fun/pallas_call | solution.py:630
  173.6 0.0 collective-permute-done.3
  173.6 0.0 collective-permute-done.4
  173.6 0.0 collective-permute-done.5
  173.7 0.0 copy-done.1
  173.7 0.1 fusion.1
  174.3 0.0 copy-start.4
  174.3 0.7 copy-done.4
Async XLA Ops:
  154.7 18.9 %collective-permute-start.3 = (bf16[64,1536]{1,0:T(8,128)(2,1)}, bf16[64,1536]{1,0:T(8,128)(2,1)S(1)}, u32[]{:S(2)}, u32[]{:S(2)}) collective-permute-start(bf16[64,1536]{1,0:T(8,128)(2,1)} %get-tuple-element.72), channel_id=1, source_target_pairs={{0,1},{1,0},{8,9},{9,8},{16,17},{17,16},{24,25},{25,24},{2,3},{3,2... | collective-permute-start | bytes 589832 | tf_op jit(solution)/shard_map/cond/branch_1_fun/ppermute | solution.py:737
  156.0 17.6 %collective-permute-start.4 = (bf16[64,1536]{1,0:T(8,128)(2,1)}, bf16[64,1536]{1,0:T(8,128)(2,1)S(1)}, u32[]{:S(2)}, u32[]{:S(2)}) collective-permute-start(bf16[64,1536]{1,0:T(8,128)(2,1)} %get-tuple-element.73), channel_id=1, source_target_pairs={{0,16},{1,17},{8,24},{9,25},{16,0},{17,1},{24,8},{25,9},{2,18},{3,... | collective-permute-start | bytes 589832 | tf_op jit(solution)/shard_map/cond/branch_1_fun/ppermute | solution.py:737
  157.5 16.1 %collective-permute-start.5 = (bf16[64,1536]{1,0:T(8,128)(2,1)}, bf16[64,1536]{1,0:T(8,128)(2,1)S(1)}, u32[]{:S(2)}, u32[]{:S(2)}) collective-permute-start(bf16[64,1536]{1,0:T(8,128)(2,1)} %get-tuple-element.74), channel_id=1, source_target_pairs={{0,17},{1,16},{8,25},{9,24},{16,1},{17,0},{24,9},{25,8},{2,19},{3,... | collective-permute-start | bytes 589832 | tf_op jit(solution)/shard_map/cond/branch_1_fun/ppermute | solution.py:737
  158.3 15.4 %copy-start.1 = (f32[64,1536]{1,0:T(8,128)S(1)}, f32[64,1536]{1,0:T(8,128)}, u32[]{:S(2)}) copy-start(f32[64,1536]{1,0:T(8,128)} %get-tuple-element.71) | copy-start | bytes 1179652 | tf_op jit(solution)/shard_map/cond
  174.3 0.7 copy-start.4
